TPU v7x, 32 devices: a whole 2x2x4 slice. The times are simulated.
32 devices in a mesh: rep: 2 (over y), grp: 8 (over z, x), sub: 2 (over core).
Axes of the slice: x: 2, y: 2, z: 4, core: 2. Of those that a mesh axis runs over, the one named last changes fastest.
Arguments:
- query_rows: bfloat16 [16, 4, 5120], P(('grp', 'sub'), 'rep'), parts along dimension 1, may hold values from -120 to 120
- cache_keys: bfloat16 [16, 4, 128, 1024], P(('grp', 'sub'), 'rep'), parts along dimension 1, may hold values from -6 to 6
- cache_values: bfloat16 [16, 4, 128, 1024], P(('grp', 'sub'), 'rep'), parts along dimension 1, may hold values from -6 to 6
- residual: bfloat16 [16, 4, 5120], P(('grp', 'sub'), 'rep'), parts along dimension 1, may hold values from -6 to 6
- lengths: int32 [16, 4], P(('grp', 'sub'), 'rep'), parts along dimension 1, may hold values from 3 to 128
- expert_ids: int32 [16, 4, 1], P(('grp', 'sub'), 'rep'), parts along dimension 1, may hold values from 0 to 3; in each aligned block of 2 rows (0 to 1, 2 to 3, ..., all dimensions but the last counted through in order) at most 2 rows name the same one
- capacity: int32 [4], replicated, may hold values from 1 to 2
- norm_gain: float32 [5120], replicated, may hold values from 0.5 to 1.5
- router: bfloat16 [5120, 4], replicated, may hold values from -0.078125 to 0.078125
- shared_gate: bfloat16 [5120, 8192], P(None, ('grp', 'sub')), may hold values from -0.078125 to 0.078125
- shared_up: bfloat16 [5120, 8192], P(None, ('grp', 'sub')), may hold values from -0.078125 to 0.078125
- shared_down: bfloat16 [8192, 5120], P(('grp', 'sub')), may hold values from -0.0625 to 0.0625
- expert_gate: bfloat16 [5120, 32768], P(None, ('grp', 'sub')), may hold values from -0.078125 to 0.078125
- expert_up: bfloat16 [5120, 32768], P(None, ('grp', 'sub')), may hold values from -0.078125 to 0.078125
- expert_down: bfloat16 [32768, 5120], P(('grp', 'sub')), may hold values from -0.0625 to 0.0625
Outputs:
- layer_out: bfloat16 [16, 4, 5120], P(('grp', 'sub'), 'rep'), parts along dimension 1
There are 2 independent parts, one for each index of `rep`. A program takes and returns all parts, laid end to end along the dimension named above; an argument that names none is the same for every part. Nothing has to cross between parts.
Inputs may be any that keep to these rules, and one draw needn't show every extreme that they name: `expert_ids`: in each aligned block of 2 rows (the rows of one device), no expert is named more than 2 times.
All inputs are finite; a program needn't handle non-finite values.
Results may differ from a plain program's by a relative error of at most 0.0075.
Values may be sent and summed in bfloat16 or wider, within the bound.
A program may use at most 128 MiB of HBM per device.

v0:
```python
import jax
import jax.numpy as jnp
from jax import lax
from jax.sharding import PartitionSpec as P

D = 5120
HEADS = 40
KV_HEADS = 8
HEAD = 128
EXPERTS = 4
EH = 8192


def attend(query_rows, cache_keys, cache_values, lengths):
    request_count = query_rows.shape[0]
    context = cache_keys.shape[1]
    groups = HEADS // KV_HEADS
    queries_f = query_rows.astype(jnp.float32).reshape(request_count, KV_HEADS, groups, HEAD)
    keys_f = cache_keys.astype(jnp.float32).reshape(request_count, context, KV_HEADS, HEAD)
    scores = jnp.einsum("rkgh,rjkh->rkgj", queries_f, keys_f) * HEAD ** (-0.5)
    key_pos = jnp.arange(context, dtype=jnp.int32)
    allowed = (key_pos[None, :] < lengths[:, None])[:, None, None, :]
    scores = jnp.where(allowed, scores, -1e30)
    row_peak = jnp.max(scores, axis=-1, keepdims=True)
    exponent = jnp.where(allowed, jnp.exp(scores - row_peak), 0.0)
    weights = (exponent / jnp.sum(exponent, axis=-1, keepdims=True)).astype(jnp.bfloat16)
    values_f = cache_values.astype(jnp.float32).reshape(request_count, context, KV_HEADS, HEAD)
    attended = jnp.einsum("rkgj,rjkh->rkgh", weights.astype(jnp.float32), values_f)
    return attended.reshape(request_count, HEADS * HEAD).astype(jnp.bfloat16)


def rms_normalize(stream, norm_gain):
    mean_square = jnp.mean(stream * stream, axis=-1, keepdims=True)
    return (stream * lax.rsqrt(mean_square + 1e-05) * norm_gain).astype(jnp.bfloat16)


def swiglu(inputs, w_gate, w_up, w_down):
    gate_part = jnp.dot(inputs, w_gate, preferred_element_type=jnp.float32)
    up_part = jnp.dot(inputs, w_up, preferred_element_type=jnp.float32)
    hidden = (jax.nn.silu(gate_part) * up_part).astype(jnp.bfloat16)
    return jnp.dot(hidden, w_down, preferred_element_type=jnp.float32)


def gated_inputs(flat_rows, router, route_ids):
    logits = jnp.dot(flat_rows, router, preferred_element_type=jnp.float32)
    onehot = route_ids[:, None] == jnp.arange(EXPERTS, dtype=jnp.int32)[None, :]
    picked = jnp.sum(jnp.where(onehot, logits, 0.0), axis=-1)
    return (flat_rows.astype(jnp.float32) * jax.nn.sigmoid(picked)[:, None]).astype(jnp.bfloat16)


def row_ranks(route_ids, capacity):
    onehot = (route_ids[:, None] == jnp.arange(EXPERTS, dtype=jnp.int32)[None, :]).astype(jnp.int32)
    before = jnp.cumsum(onehot, axis=0) - onehot
    row_rank = jnp.sum(before * onehot, axis=1)
    row_limit = jnp.sum(onehot * capacity[None, :], axis=1)
    return (row_rank, row_rank < row_limit)


def per_device(
    query_rows,
    cache_keys,
    cache_values,
    residual,
    lengths,
    expert_ids,
    capacity,
    norm_gain,
    router,
    shared_gate,
    shared_up,
    shared_down,
    expert_gate,
    expert_up,
    expert_down,
):
    tok_count = query_rows.shape[1]
    attended = attend(query_rows[0], cache_keys[0], cache_values[0], lengths[0])
    stream = residual[0].astype(jnp.float32) + attended.astype(jnp.float32)
    flat_rows = rms_normalize(stream, norm_gain)
    route_ids = expert_ids[0].reshape(tok_count)
    gathered, all_ids = (
        lax.all_gather(flat_rows, ("grp", "sub"), axis=0, tiled=True),
        lax.all_gather(route_ids, ("grp", "sub"), axis=0, tiled=True),
    )
    all_scaled = gated_inputs(gathered, router, all_ids)
    rank_unused, kept_all = jax.vmap(row_ranks, in_axes=(0, None))(
        all_ids.reshape(-1, tok_count), capacity
    )
    own_expert = lax.axis_index(("grp", "sub")) * expert_gate.shape[1] // EH
    usable = (all_ids == own_expert) & kept_all.reshape(-1)
    masked = jnp.where(usable[:, None], all_scaled, jnp.zeros_like(all_scaled))
    shared_part = swiglu(gathered, shared_gate, shared_up, shared_down)
    branch_sum = lax.psum_scatter(
        shared_part + swiglu(masked, expert_gate, expert_up, expert_down),
        ("grp", "sub"),
        scatter_dimension=0,
        tiled=True,
    )
    layer_out = stream + branch_sum
    return layer_out.astype(jnp.bfloat16).reshape(1, tok_count, D)


def solution(mesh):
    placed = (
        P(("grp", "sub"), "rep", None),
        P(("grp", "sub"), "rep", None, None),
        P(("grp", "sub"), "rep", None, None),
        P(("grp", "sub"), "rep", None),
        P(("grp", "sub"), "rep"),
        P(("grp", "sub"), "rep", None),
        P(),
        P(),
        P(),
        P(None, ("grp", "sub")),
        P(None, ("grp", "sub")),
        P(("grp", "sub"), None),
        P(None, ("grp", "sub")),
        P(None, ("grp", "sub")),
        P(("grp", "sub"), None),
    )
    return jax.shard_map(
        per_device,
        mesh=mesh,
        in_specs=placed,
        out_specs=P(("grp", "sub"), "rep", None),
        check_vma=False,
    )
```

profile of v0, /device:TPU:0, one launch (start us, length us, event | category | flops | bytes accessed | tf_op | source)
XLA Modules:
  0.0 184.4 jit_solution(740923644199911297)
XLA Ops:
  6.5 1.4 fusion.38
  8.6 0.8 bitcast_dynamic-update-slice_fusion
  9.4 13.7 %all-reduce = s32[32]{0:T(128)S(1)} all-reduce(s32[32]{0:T(128)S(1)} %bitcast_dynamic-update-slice_fusion), channel_id=2, replica_groups=mesh['rep'=2,'grp'=8,'sub'=2] {'grp','sub'}, use_global_device_ids=true, to_apply=%add | all-reduce | flops 32 | bytes 256 | tf_op jit(solution)/shard_map/all_gather | solution.py:83
  23.3 0.7 select_reduce_fusion
  24.1 0.1 copy.25
  24.2 0.1 lt.31
  24.3 0.7 iota_compare_fusion.3
  25.0 1.1 copy.26
  26.1 0.8 reshape.66
  26.9 0.4 fusion.5
  27.3 0.2 fusion.39
  27.5 1.1 copy.27
  28.6 0.3 fusion.7
  29.0 0.9 multiply_reduce_fusion
  29.9 0.8 fusion.29
  30.7 18.8 %all-gather.1 = bf16[16,2,5120]{2,1,0:T(2,128)(2,1)S(1)} all-gather(bf16[1,2,5120]{2,1,0:T(2,128)(2,1)S(1)} %fusion.29), channel_id=1, replica_groups=mesh['rep'=2,'grp'=8,'sub'=2] {'grp','sub'}, dimensions={0}, use_global_device_ids=true | all-gather | bytes 348160 | tf_op jit(solution)/shard_map/all_gather | solution.py:82
  49.6 0.1 reshape.78
  49.7 0.2 fusion.9
  49.9 3.5 %fusion.41 = f32[32,512]{1,0:T(8,128)S(1)} fusion(bf16[32,5120]{1,0:T(8,128)(2,1)S(1)} %reshape.78, bf16[5120,512]{1,0:T(8,128)(2,1)} %param.24), kind=kOutput, calls=%fused_computation.59 | convolution fusion | flops 167772160 | bytes 5636096 | tf_op jit(solution)/shard_map/dot_general | solution.py:38
  53.4 8.9 %fusion.36 = f32[32,2048]{1,0:T(8,128)S(1)} fusion(bf16[5120,2048]{1,0:T(8,128)(2,1)} %param.27, bf16[32,5120]{1,0:T(8,128)(2,1)S(1)} %reshape.78, f32[32]{0:T(128)S(1)} %add_divide_fusion, pred[32]{0:T(512)(128)(4,1)S(1)} %compare_and_fusion), kind=kOutput, calls=%fused_computation.55 | convolution fusion | flops 671744000 | bytes 21561504 | tf_op jit(solution)/shard_map/dot_general | solution.py:38
  62.4 16.8 %fusion.10 = f32[32,5120]{1,0:T(8,128)S(1)} fusion(bf16[2048,5120]{1,0:T(8,128)(2,1)} %param.29, bf16[5120,2048]{1,0:T(8,128)(2,1)} %param.28, f32[32,2048]{1,0:T(8,128)S(1)} %fusion.36, bf16[32,5120]{1,0:T(8,128)(2,1)S(1)} %reshape.78, f32[32]{0:T(128)S(1)} %add_divide_fusion, pred[32]{0:T(512)(128)(4,1)S(1)} %compare_and_fusion), kind=kOutput, calls=%fused_computation.18 | convolution fusion | flops 1343225856 | bytes 43188384 | tf_op jit(solution)/shard_map/dot_general | solution.py:41
  79.2 6.9 %convolution_add_fusion = f32[32,5120]{1,0:T(8,128)} fusion(f32[32,5120]{1,0:T(8,128)S(1)} %fusion.10, bf16[512,5120]{1,0:T(8,128)(2,1)} %param.26, bf16[32,5120]{1,0:T(8,128)(2,1)S(1)} %reshape.78, bf16[5120,512]{1,0:T(8,128)(2,1)} %param.25, f32[32,512]{1,0:T(8,128)S(1)} %fusion.41), kind=kOutput, calls=%fused_computation.1 | convolution fusion | flops 335806464 | bytes 12189696 | tf_op jit(solution)/shard_map/dot_general | solution.py:41
  86.8 89.3 %all-reduce.4.cloned.1.call-done = f32[32,5120]{1,0:T(8,128)} async-done(((f32[32,5120]{1,0:T(8,128)}), f32[32,5120]{1,0:T(8,128)}) %all-reduce.4.cloned.1.call-update) | async-done | bytes 655376
  176.0 1.6 fusion.28
  (17 shorter events, 0.3 us)
Async XLA Ops:
  6.5 43.2 %copy-start = (bf16[5120,4]{0,1:T(4,128)(2,1)S(1)}, bf16[5120,4]{0,1:T(4,128)(2,1)}, u32[]{:S(2)}) copy-start(bf16[5120,4]{0,1:T(4,128)(2,1)} %param.23) | copy-start | bytes 122884
  6.5 169.5 %all-reduce.4.cloned.1.call-start = ((), (), s32[]{:S(2)}) async-start(), calls=%async_computation | async-start | bytes 1310720
  62.4 113.6 %copy-start.2 = (bf16[1,2,5120]{2,1,0:T(2,128)(2,1)S(1)}, bf16[1,2,5120]{2,1,0:T(2,128)(2,1)}, u32[]{:S(2)}) copy-start(bf16[1,2,5120]{2,1,0:T(2,128)(2,1)} %param.18) | copy-start | bytes 61444
  62.4 115.2 %copy-start.1 = (bf16[5120,4]{0,1:T(4,128)(2,1)S(1)}, bf16[5120,4]{0,1:T(4,128)(2,1)}, u32[]{:S(2)}) copy-start(bf16[5120,4]{0,1:T(4,128)(2,1)} %param.23) | copy-start | bytes 122884
Sparse Core Ops, SparseCore 0:
  86.2 89.7 all-reduce.3
where the time goes:
time: 185 us; the launch traced here: 184 us
  waiting for transfers between devices  89.3 us (48%)
  matrix products  37 us (20%)
  blocking collectives  32.6 us (18%)
  between operations  14.8 us (8%)
  local copies, waits for them, and re-layouts  5.71 us (3%)
  other arithmetic  5.03 us (3%)
    unnamed x2, waiting for transfers between devices  89.3 us
    dot_general x2, matrix products, swiglu(): return jnp.dot(hidden, w_down, preferred_element_type=jnp.float32)  23.7 us
    all_gather x1, blocking collectives, per_device(): lax.all_gather(flat_rows, ('grp', 'sub'), axis=0, tiled=True)  18.8 us
    all_gather x1, blocking collectives, per_device(): lax.all_gather(route_ids, ('grp', 'sub'), axis=0, tiled=True)  13.7 us
    dot_general x2, matrix products, swiglu(): gate_part = jnp.dot(inputs, w_gate, preferred_element_type=jnp.float32)  12.4 us
    unnamed x12, local copies, waits for them, and re-layouts  4.56 us
  transfers between devices with their start and end apart: 1, of which 1 were waited for; matrix products, arithmetic and copies ran while one was open for 0% of the time, Pallas kernels for 0%

commit v1 on v0

--- a/solution.py
+++ b/solution.py
@@ -79,7 +79,12 @@
     flat_rows = rms_normalize(stream, norm_gain)
     route_ids = expert_ids[0].reshape(tok_count)
     gathered, all_ids = (
-        lax.all_gather(flat_rows, ("grp", "sub"), axis=0, tiled=True),
+        jnp.concatenate(
+            lax.all_to_all(
+                jnp.stack([flat_rows] * lax.axis_size(("grp", "sub"))), ("grp", "sub"), 0, 0
+            ),
+            axis=0,
+        ),
         lax.all_gather(route_ids, ("grp", "sub"), axis=0, tiled=True),
     )
     all_scaled = gated_inputs(gathered, router, all_ids)

time: 185 us -> 173 us (0.935)
  blocking collectives: 32.6 us -> 12.4 us
  starting transfers between devices: 0.01 us -> 7.43 us
    all_gather x1 -> x0, blocking collectives: 18.8 us -> none  [per_device(): lax.all_gather(flat_rows, ('grp', 'sub'), axis=0, tiled=True)]
    all_to_all x0 -> x1, starting transfers between devices: none -> 7.39 us  [per_device(): lax.all_to_all(jnp.stack([flat_rows] * lax.axis_size(('grp', 'sub'))), ('...]
    unnamed x12 -> x11, local copies, waits for them, and re-layouts: 4.56 us -> 4.44 us
  transfers between devices with their start and end apart: 1 -> 2, of which waited for: 1 -> 1; matrix products, arithmetic and copies ran while one was open for 0% -> 2% of each run, Pallas kernels for 0% -> 0%
where the time goes in v1:
time: 173 us; the launch traced here: 172 us
  waiting for transfers between devices  88.9 us (51%)
  matrix products  37 us (21%)
  between operations  14.9 us (9%)
  blocking collectives  12.4 us (7%)
  starting transfers between devices  7.43 us (4%)
  local copies, waits for them, and re-layouts  6.63 us (4%)
  other arithmetic  5.03 us (3%)
    unnamed x2, waiting for transfers between devices  88.9 us
    dot_general x2, matrix products, swiglu(): return jnp.dot(hidden, w_down, preferred_element_type=jnp.float32)  23.7 us
    dot_general x2, matrix products, swiglu(): gate_part = jnp.dot(inputs, w_gate, preferred_element_type=jnp.float32)  12.4 us
    all_gather x1, blocking collectives, per_device(): lax.all_gather(route_ids, ('grp', 'sub'), axis=0, tiled=True)  12.4 us
    all_to_all x1, starting transfers between devices, per_device(): lax.all_to_all(jnp.stack([flat_rows] * lax.axis_size(('grp', 'sub'))), ('...  7.39 us
    unnamed x11, local copies, waits for them, and re-layouts  4.44 us
  transfers between devices with their start and end apart: 2, of which 1 were waited for; matrix products, arithmetic and copies ran while one was open for 2% of the time, Pallas kernels for 0%

profile of v1, /device:TPU:0, one launch (start us, length us, event | category | flops | bytes accessed | tf_op | source)
XLA Modules:
  0.0 172.3 jit_solution(8611515049066876271)
XLA Ops:
  6.5 0.7 iota_compare_fusion.3
  7.3 1.1 copy.26
  8.4 0.8 reshape.99
  9.2 0.4 fusion.5
  9.5 0.2 fusion.43
  9.7 1.1 copy.27
  10.9 0.3 fusion.7
  11.3 0.9 multiply_reduce_fusion
  12.2 0.8 fusion.33
  13.0 0.9 stack.5
  13.9 7.4 %all-to-all-start = ((bf16[16,2,5120]{2,1,0:T(2,128)(2,1)}), bf16[16,2,5120]{2,1,0:T(2,128)(2,1)S(1)}, u32[]{:S(2)}, u32[]{:S(2)}) async-start(bf16[16,2,5120]{2,1,0:T(2,128)(2,1)} %stack.5), calls=%async_computation | async-start | bytes 655360 | tf_op jit(solution)/shard_map/all_to_all | solution.py:83
  21.3 1.4 fusion.42
  23.5 0.8 bitcast_dynamic-update-slice_fusion
  24.2 12.4 %all-reduce = s32[32]{0:T(128)S(1)} all-reduce(s32[32]{0:T(128)S(1)} %bitcast_dynamic-update-slice_fusion), channel_id=2, replica_groups=mesh['rep'=2,'grp'=8,'sub'=2] {'grp','sub'}, use_global_device_ids=true, to_apply=%add | all-reduce | flops 32 | bytes 256 | tf_op jit(solution)/shard_map/all_gather | solution.py:88
  36.7 0.8 select_reduce_fusion
  37.5 0.1 copy.25
  37.8 0.1 reshape.102
  37.9 0.2 fusion.9
  38.1 3.5 %fusion.45 = f32[32,512]{1,0:T(8,128)S(1)} fusion(bf16[32,5120]{1,0:T(8,128)(2,1)S(1)} %reshape.102, bf16[5120,512]{1,0:T(8,128)(2,1)} %param.24), kind=kOutput, calls=%fused_computation.63 | convolution fusion | flops 167772160 | bytes 5636096 | tf_op jit(solution)/shard_map/dot_general | solution.py:38
  41.6 8.9 %fusion.40 = f32[32,2048]{1,0:T(8,128)S(1)} fusion(bf16[5120,2048]{1,0:T(8,128)(2,1)} %param.27, bf16[32,5120]{1,0:T(8,128)(2,1)S(1)} %reshape.102, f32[32]{0:T(128)S(1)} %add_divide_fusion, pred[32]{0:T(512)(128)(4,1)S(1)} %compare_and_fusion), kind=kOutput, calls=%fused_computation.59 | convolution fusion | flops 671744000 | bytes 21561504 | tf_op jit(solution)/shard_map/dot_general | solution.py:38
  50.6 16.8 %fusion.10 = f32[32,5120]{1,0:T(8,128)S(1)} fusion(bf16[2048,5120]{1,0:T(8,128)(2,1)} %param.29, bf16[5120,2048]{1,0:T(8,128)(2,1)} %param.28, f32[32,2048]{1,0:T(8,128)S(1)} %fusion.40, bf16[32,5120]{1,0:T(8,128)(2,1)S(1)} %reshape.102, f32[32]{0:T(128)S(1)} %add_divide_fusion, pred[32]{0:T(512)(128)(4,1)S(1)} %compare_and_fusion), kind=kOutput, calls=%fused_computation.18 | convolution fusion | flops 1343225856 | bytes 43188384 | tf_op jit(solution)/shard_map/dot_general | solution.py:41
  67.4 6.9 %convolution_add_fusion = f32[32,5120]{1,0:T(8,128)} fusion(f32[32,5120]{1,0:T(8,128)S(1)} %fusion.10, bf16[512,5120]{1,0:T(8,128)(2,1)} %param.26, bf16[32,5120]{1,0:T(8,128)(2,1)S(1)} %reshape.102, bf16[5120,512]{1,0:T(8,128)(2,1)} %param.25, f32[32,512]{1,0:T(8,128)S(1)} %fusion.45), kind=kOutput, calls=%fused_computation.1 | convolution fusion | flops 335806464 | bytes 12189696 | tf_op jit(solution)/shard_map/dot_general | solution.py:41
  74.9 88.9 %all-reduce.4.cloned.1.call-done = f32[32,5120]{1,0:T(8,128)} async-done(((f32[32,5120]{1,0:T(8,128)}), f32[32,5120]{1,0:T(8,128)}) %all-reduce.4.cloned.1.call-update) | async-done | bytes 655376
  163.9 1.6 fusion.32
  (20 shorter events, 0.5 us)
Async XLA Ops:
  6.5 31.4 %copy-start = (bf16[5120,4]{0,1:T(4,128)(2,1)S(1)}, bf16[5120,4]{0,1:T(4,128)(2,1)}, u32[]{:S(2)}) copy-start(bf16[5120,4]{0,1:T(4,128)(2,1)} %param.23) | copy-start | bytes 122884
  13.9 23.9 %all-to-all-start = ((bf16[16,2,5120]{2,1,0:T(2,128)(2,1)}), bf16[16,2,5120]{2,1,0:T(2,128)(2,1)S(1)}, u32[]{:S(2)}, u32[]{:S(2)}) async-start(bf16[16,2,5120]{2,1,0:T(2,128)(2,1)} %stack.5), calls=%async_computation | async-start | bytes 655360 | tf_op jit(solution)/shard_map/all_to_all | solution.py:83
  21.3 142.6 %all-reduce.4.cloned.1.call-start = ((), (), s32[]{:S(2)}) async-start(), calls=%async_computation.1 | async-start | bytes 1310720
  50.6 113.3 %copy-start.2 = (bf16[1,2,5120]{2,1,0:T(2,128)(2,1)S(1)}, bf16[1,2,5120]{2,1,0:T(2,128)(2,1)}, u32[]{:S(2)}) copy-start(bf16[1,2,5120]{2,1,0:T(2,128)(2,1)} %param.18) | copy-start | bytes 61444
  50.6 114.9 %copy-start.1 = (bf16[5120,4]{0,1:T(4,128)(2,1)S(1)}, bf16[5120,4]{0,1:T(4,128)(2,1)}, u32[]{:S(2)}) copy-start(bf16[5120,4]{0,1:T(4,128)(2,1)} %param.23) | copy-start | bytes 122884
Sparse Core Ops, SparseCore 0:
  74.4 89.3 all-reduce.3
